TPU v7x, 32 devices: a whole 2x2x4 slice. The times are simulated.
32 devices in a mesh: group: 2 (over x), ctx: 8 (over z, y), tp: 2 (over core).
Axes of the slice: x: 2, y: 2, z: 4, core: 2. Of those that a mesh axis runs over, the one named last changes fastest.
Arguments:
- query_proj: bfloat16 [2048, 8192], P(('group', 'ctx'), 'tp'), parts along dimension 0, may hold values from -6 to 6
- key_proj: bfloat16 [2048, 8192], P(('group', 'ctx'), 'tp'), parts along dimension 0, may hold values from -6 to 6
- value_proj: bfloat16 [2048, 8192], P(('group', 'ctx'), 'tp'), parts along dimension 0, may hold values from -6 to 6
- genome_ids: int32 [2048], P('group'), parts along dimension 0, may hold values from 0 to 3, never falling along the last dimension, each value on 1 to 512 neighbouring positions
- filters: float32 [512, 128], P('tp'), may hold values from -0.5 to 0.5
- out_weight: bfloat16 [8192, 8192], P('tp', 'ctx'), may hold values from -0.0625 to 0.0625
- out_grad: bfloat16 [2048, 8192], P(('group', 'ctx'), 'tp'), parts along dimension 0, may hold values from -6 to 6
Outputs:
- query_grad: bfloat16 [2048, 8192], P(('group', 'ctx'), 'tp'), parts along dimension 0
- key_grad: bfloat16 [2048, 8192], P(('group', 'ctx'), 'tp'), parts along dimension 0
- value_grad: bfloat16 [2048, 8192], P(('group', 'ctx'), 'tp'), parts along dimension 0
- filter_grad: float32 [1024, 128], P(('group', 'tp')), parts along dimension 0
There are 2 independent parts, one for each index of `group`. A program takes and returns all parts, laid end to end along the dimension named above; an argument that names none is the same for every part. Nothing has to cross between parts.
Inputs may be any that keep to these rules, and one draw needn't show every extreme that they name: `genome_ids`: genome ids never fall along the rows; every genome covers 1 to 512 consecutive rows, and one covers exactly 512.
All inputs are finite; a program needn't handle non-finite values.
Results may differ from a plain program's by a relative error of at most 0.017.
Values may be sent and summed in bfloat16 or wider, within the bound.
A program may use at most 192 MiB of HBM per device.

v0:
```python
import jax
import jax.numpy as jnp
import numpy as np
from jax import lax
from jax.sharding import PartitionSpec as P


def from_behind(array, axis, by):
    length = lax.axis_size(axis)
    pairs = [(i, i + by) for i in range(length) if 0 <= i + by < length]
    return lax.ppermute(array, axis, pairs)


def rounded(source):
    return lax.optimization_barrier(source.astype(jnp.bfloat16)).astype(jnp.float32)


def lag_tables(filt_vals, tap_count):
    row_pos = np.arange(tap_count)[:, None]
    col_pos = np.arange(2 * tap_count)[None, :]
    tables = []
    for offsets in (row_pos + tap_count - col_pos, col_pos - row_pos):
        inside = (offsets >= 0) & (offsets < tap_count)
        picked = jnp.take(filt_vals, np.clip(offsets, 0, tap_count - 1).reshape(-1), axis=1)
        picked = picked.reshape(filt_vals.shape[0], tap_count, 2 * tap_count)
        tables.append(jnp.where(inside[None], picked, jnp.zeros_like(picked)))
    return (tables[0], tables[1])


def fold_lags(product, tap_count):
    group_count = product.shape[0]
    flat = product.reshape(group_count, 2 * tap_count * tap_count)
    flat = jnp.concatenate([flat, jnp.zeros((group_count, tap_count), flat.dtype)], 1)
    skewed = flat.reshape(group_count, tap_count, 2 * tap_count + 1)
    return jnp.flip(jnp.sum(skewed[:, :, 1 : tap_count + 1], axis=1), axis=1)


def per_device(query_proj, key_proj, value_proj, genome_ids, filters, out_weight, out_grad):
    row_count, feature_count = query_proj.shape
    group_local = filters.shape[0]
    chan_count = feature_count // group_local
    tap_count = filters.shape[1]
    first_global = lax.axis_index("ctx") * row_count
    pad_ids = jnp.full((tap_count,), -1, jnp.int32)
    ids_pad = jnp.concatenate([pad_ids, genome_ids, pad_ids])
    key_f32 = key_proj.astype(jnp.float32)
    value_f32 = value_proj.astype(jnp.float32)
    mixed = (key_f32 * value_f32).astype(jnp.bfloat16)
    before = from_behind(mixed, "ctx", 1)
    mixed_ext = jnp.concatenate([before, mixed], 0)
    fwd_table, back_table = lag_tables(filters.astype(jnp.bfloat16), tap_count)
    grad_full = lax.all_gather(out_grad, "tp", axis=1, tiled=True)
    columns = lax.all_to_all(grad_full, "ctx", split_axis=1, concat_axis=0, tiled=True)
    summed = lax.psum_scatter(
        lax.dot_general(
            columns, out_weight, (((1,), (1,)), ((), ())), preferred_element_type=jnp.float32
        ).astype(jnp.bfloat16),
        "ctx",
        scatter_dimension=0,
        tiled=True,
    ).astype(jnp.float32)
    dz_vals = rounded(summed)
    block_index = 0
    first_row = block_index * tap_count
    window = mixed_ext
    ids_rows = lax.dynamic_slice_in_dim(ids_pad, first_global + first_row + tap_count, tap_count)
    ids_prev = lax.dynamic_slice_in_dim(ids_pad, first_global + first_row, 2 * tap_count)
    ids_next = lax.dynamic_slice_in_dim(
        ids_pad, first_global + first_row + tap_count, 2 * tap_count
    )
    same_prev = (ids_rows[:, None] == ids_prev[None, :]).astype(jnp.bfloat16)
    prev_masks = [same_prev]
    next_masks = [(ids_rows[:, None] == ids_next[None, :]).astype(jnp.bfloat16)]
    block_out = jnp.einsum(
        "gtw,wgc->tgc",
        fwd_table * same_prev[None],
        window.reshape(2 * tap_count, group_local, chan_count),
        preferred_element_type=jnp.float32,
    )
    conv_parts = block_out.reshape(tap_count, feature_count)
    query_grad = (dz_vals * conv_parts).astype(jnp.bfloat16)
    grad_conv = (dz_vals * query_proj.astype(jnp.float32)).astype(jnp.bfloat16)
    after = from_behind(grad_conv, "ctx", -1)
    grad_ext = jnp.concatenate([grad_conv, after], 0)
    block_index = 0
    window = mixed_ext.reshape(2 * tap_count, group_local, chan_count)
    grad_window = grad_ext.reshape(2 * tap_count, group_local, chan_count)
    grad_rows = grad_conv.reshape(tap_count, group_local, chan_count)
    block_grad = jnp.einsum(
        "gtw,wgc->tgc",
        back_table * next_masks[block_index][None],
        grad_window,
        preferred_element_type=jnp.float32,
    )
    grad_parts = block_grad.reshape(tap_count, feature_count)
    product = jnp.einsum("tgc,wgc->gtw", grad_rows, window, preferred_element_type=jnp.float32)
    filt_local = fold_lags(product * prev_masks[block_index].astype(jnp.float32)[None], tap_count)
    key_grad = (grad_parts * value_f32).astype(jnp.bfloat16)
    value_grad = (grad_parts * key_f32).astype(jnp.bfloat16)
    filter_grad = lax.psum(filt_local.astype(jnp.bfloat16), "ctx").astype(jnp.float32)
    return (query_grad, key_grad, value_grad, filter_grad)


def solution(mesh):
    in_specs = (
        P(("group", "ctx"), "tp"),
        P(("group", "ctx"), "tp"),
        P(("group", "ctx"), "tp"),
        P("group"),
        P("tp", None),
        P("tp", "ctx"),
        P(("group", "ctx"), "tp"),
    )
    out_specs = (
        P(("group", "ctx"), "tp"),
        P(("group", "ctx"), "tp"),
        P(("group", "ctx"), "tp"),
        P(("group", "tp"), None),
    )
    return jax.shard_map(
        per_device, mesh=mesh, in_specs=in_specs, out_specs=out_specs, check_vma=False
    )
```

profile of v0, /device:TPU:0, one launch (start us, length us, event | category | flops | bytes accessed | tf_op | source)
XLA Modules:
  0.0 785.1 jit_solution(3224054432893824704)
XLA Ops:
  7.2 0.0 all-gather.2.cloned.1.call-start
  7.2 2.3 copy.46
  9.5 0.0 all-gather.2.cloned.1.call-update
  9.5 0.0 reduce-scatter.2.cloned.1.call-start
  9.5 13.9 %all-gather.2.cloned.1.call-done = bf16[128,8192]{0,1:T(8,128)(2,1)} async-done(((bf16[128,4096]{0,1:T(8,128)(2,1)}), bf16[128,8192]{0,1:T(8,128)(2,1)}) %all-gather.2.cloned.1.call-update) | async-done | bytes 2097168 | tf_op jit(solution)/shard_map/all_gather | solution.py:52
  23.4 54.4 %all_to_all.19 = bf16[128,8,1024]{0,2,1:T(8,128)(2,1)S(1)} all-to-all(bf16[128,8,1024]{0,2,1:T(8,128)(2,1)} %bitcast.34), channel_id=1, replica_groups=mesh['group'=2,'ctx'=8,'tp'=2] {'ctx'}, dimensions={1} | all-to-all | bytes 4194304 | tf_op jit(solution)/shard_map/all_to_all | solution.py:53
  77.9 2.7 copy.47
  80.5 14.8 %convolution_convert_fusion = bf16[1024,4096]{1,0:T(8,128)(2,1)} fusion(bf16[1024,1024]{1,0:T(8,128)(2,1)} %bitcast.38, bf16[4096,1024]{1,0:T(8,128)(2,1)} %param.18), kind=kOutput, calls=%fused_computation.16 | convolution fusion | flops 8594128896 | bytes 18874368 | tf_op jit(solution)/shard_map/dot_general | solution.py:55
  95.3 0.0 copy-start.7
  95.3 0.0 copy-start.3
  95.3 0.0 copy-start.2
  95.3 0.0 copy-start.5
  95.3 0.0 reduce-scatter.2.cloned.1.call-update
  95.4 0.0 all-reduce.3.cloned.1.call-start
  95.4 0.7 copy-done.7
  96.1 0.1 copy-done.3
  96.2 0.1 copy.49
  96.4 147.2 %reduce-scatter.2.cloned.1.call-done = bf16[128,4096]{1,0:T(8,128)(2,1)} async-done(((bf16[1024,4096]{1,0:T(8,128)(2,1)}), bf16[128,4096]{1,0:T(8,128)(2,1)}) %reduce-scatter.2.cloned.1.call-update) | async-done | bytes 1048592 | tf_op jit(solution)/shard_map/reduce_scatter | solution.py:54
  243.5 0.0 copy-done.2
  243.5 1.5 fusion.13
  245.0 1.3 collective-permute-start.1
  246.3 0.0 copy-done.5
  246.4 129.4 %gather_fusion.1 = bf16[32768,256]{1,0:T(8,128)(2,1)} fusion(bf16[256,128]{0,1:T(8,128)(2,1)S(1)} %copy.49, s32[32768]{0:T(1024)S(1)} %broadcast_clamp_fusion), kind=kCustom, calls=%fused_computation.1.clone | custom fusion | bytes 33685504 | tf_op jit(solution)/shard_map/jit(_take)/gather | solution.py:24
  375.8 0.0 copy-start.8
  375.8 23.5 %copy.53 = bf16[256,128,256]{2,1,0:T(8,128)(2,1)} copy(bf16[256,128,256]{0,2,1:T(8,128)(2,1)} %bitcast.29) | data formatting | bytes 33554432 | tf_op jit(solution)/shard_map/reshape | solution.py:25
  399.3 0.0 copy-done.8
  399.3 0.1 dynamic_slice.9
  399.4 0.1 fusion.20
  399.5 0.1 fusion.17
  399.6 0.0 collective-permute-done.1
  399.6 1.4 pad_maximum_fusion.1
  401.0 2.5 copy.52
  403.4 12.2 %fusion = f32[256,16,128]{2,1,0:T(8,128)} fusion(bf16[256,256,16]{0,2,1:T(8,128)(2,1)} %bitcast.35, bf16[256,128,256]{2,1,0:T(8,128)(2,1)} %copy.53, pred[128,256]{1,0:T(8,128)(4,1)S(1)} %copy.61, bf16[128,256]{1,0:T(8,128)(2,1)S(1)} %get-tuple-element.16), kind=kOutput, calls=%fused_computation.4 | convolution fusion | flops 285212672 | bytes 21069824 | tf_op jit(solution)/shard_map/gtw,wgc->tgc/dot_general | solution.py:89
  415.6 1.9 copy.54
  417.6 0.0 copy-start.6
  417.6 0.0 copy-start.4
  417.6 3.7 fusion.14
  421.3 5.5 collective-permute-start
  426.9 0.0 copy-done.6
  426.9 0.0 copy-done.4
  426.9 129.4 %gather_fusion = bf16[32768,256]{1,0:T(8,128)(2,1)} fusion(bf16[256,128]{0,1:T(8,128)(2,1)S(1)} %copy.49, s32[32768]{0:T(1024)S(1)} %broadcast_clamp_fusion.1), kind=kCustom, calls=%fused_computation.clone | custom fusion | bytes 33685504 | tf_op jit(solution)/shard_map/jit(_take)/gather | solution.py:24
  556.4 23.5 %copy.50 = bf16[256,128,256]{2,1,0:T(8,128)(2,1)} copy(bf16[256,128,256]{0,2,1:T(8,128)(2,1)} %bitcast.28) | data formatting | bytes 33554432 | tf_op jit(solution)/shard_map/reshape | solution.py:25
  579.8 0.7 copy.56
  580.5 0.0 collective-permute-done
  580.5 3.1 pad_maximum_fusion
  583.6 3.3 copy.48
  586.9 11.6 %fusion.3 = f32[256,16,128]{2,1,0:T(8,128)} fusion(bf16[256,256,16]{0,2,1:T(8,128)(2,1)S(1)} %bitcast.30, bf16[256,128,256]{2,1,0:T(8,128)(2,1)} %copy.50, pred[128,256]{1,0:T(8,128)(4,1)S(1)} %copy.62, bf16[128,256]{1,0:T(8,128)(2,1)S(1)} %get-tuple-element.15), kind=kOutput, calls=%fused_computation.7 | convolution fusion | flops 285212672 | bytes 21069824 | tf_op jit(solution)/shard_map/gtw,wgc->tgc/dot_general | solution.py:74
  598.5 3.0 copy.51
  601.5 13.1 %broadcast_multiply_fusion = f32[256,128,256]{2,1,0:T(8,128)} fusion(f32[128,256]{1,0:T(8,128)S(1)} %get-tuple-element.14, bf16[128,256,16]{0,2,1:T(8,128)(2,1)S(1)} %bitcast.33, bf16[256,256,16]{0,2,1:T(8,128)(2,1)S(1)} %bitcast.31), kind=kOutput, calls=%fused_computation.3 | convolution fusion | flops 276824064 | bytes 36831232 | tf_op jit(solution)/shard_map/tgc,wgc->gtw/dot_general | solution.py:96
  614.6 35.0 %copy.59 = f32[256,128,256]{0,2,1:T(8,128)} copy(f32[256,128,256]{2,1,0:T(8,128)} %broadcast_multiply_fusion) | data formatting | bytes 67108864 | tf_op jit(solution)/shard_map/reshape | solution.py:32
  649.6 22.4 %concatenate.15 = f32[256,32896]{0,1:T(8,128)} pad(f32[256,32768]{0,1:T(8,128)} %bitcast.27, f32[]{:T(128)} %constant.38.clone.1), padding=0_0x0_128 | pad | bytes 67239936 | tf_op jit(solution)/shard_map/concatenate | solution.py:33
  672.0 28.3 %reshape.129 = f32[256,128,257]{0,2,1:T(8,128)} reshape(f32[256,32896]{0,1:T(8,128)} %concatenate.15) | data formatting | bytes 67371008 | tf_op jit(solution)/shard_map/reshape | solution.py:34
  700.2 0.0 copy-start
  700.2 0.0 copy-start.1
  700.3 8.4 %slice_reduce_fusion = bf16[256,128]{0,1:T(8,128)(2,1)S(1)} fusion(f32[256,128,257]{0,2,1:T(8,128)} %reshape.129), kind=kLoop, calls=%fused_computation.2 | loop fusion | flops 4161536 | bytes 16842752 | tf_op jit(solution)/shard_map/reduce_sum | solution.py:35
  708.6 0.7 rev.4
  709.3 0.0 all-reduce.3.cloned.1.call-update
  709.3 0.0 copy-done
  709.3 0.0 copy-done.1
  709.3 1.2 fusion.12
  710.5 66.4 %all-reduce.3.cloned.1.call-done = bf16[256,128]{0,1:T(8,128)(2,1)} async-done(((bf16[256,128]{0,1:T(8,128)(2,1)}), bf16[256,128]{0,1:T(8,128)(2,1)}) %all-reduce.3.cloned.1.call-update) | async-done | bytes 65552 | tf_op jit(solution)/shard_map/psum | solution.py:100
  776.9 1.6 copy.58
  (6 shorter events, 0.1 us)
Async XLA Ops:
  7.2 16.3 %all-gather.2.cloned.1.call-start = ((), (), s32[]{:S(2)}) async-start(), calls=%async_computation.2 | async-start | bytes 3145728 | tf_op jit(solution)/shard_map/all_gather | solution.py:52
  9.5 234.0 %reduce-scatter.2.cloned.1.call-start = ((), (), s32[]{:S(2)}) async-start(), calls=%async_computation.3 | async-start | bytes 9437184 | tf_op jit(solution)/shard_map/reduce_scatter | solution.py:54
  95.3 0.8 copy-start.7
  95.3 0.9 copy-start.3
  95.3 148.2 %copy-start.2 = (bf16[128,4096]{1,0:T(8,128)(2,1)S(1)}, bf16[128,4096]{1,0:T(8,128)(2,1)}, u32[]{:S(2)}) copy-start(bf16[128,4096]{1,0:T(8,128)(2,1)} %param.13) | copy-start | bytes 3145732
  95.3 151.0 %copy-start.5 = (s32[32768]{0:T(1024)S(1)}, s32[32768]{0:T(1024)}, u32[]{:S(2)}) copy-start(s32[32768]{0:T(1024)} %constant.66) | copy-start | bytes 393220
  95.4 681.6 %all-reduce.3.cloned.1.call-start = ((), (), s32[]{:S(2)}) async-start(), calls=%async_computation.4 | async-start | bytes 131072 | tf_op jit(solution)/shard_map/psum | solution.py:100
  245.0 154.6 %collective-permute-start.1 = (bf16[128,4096]{1,0:T(8,128)(2,1)S(1)}, bf16[128,4096]{1,0:T(8,128)(2,1)}, u32[]{:S(2)}, u32[]{:S(2)}) collective-permute-start(bf16[128,4096]{1,0:T(8,128)(2,1)S(1)} %fusion.13), channel_id=1, source_target_pairs={{2,0},{4,2},{6,4},{8,6},{10,8},{12,10},{14,12},{3,1},{5,3},{7,5},{... | collective-permute-start | bytes 3145736 | tf_op jit(solution)/shard_map/ppermute | solution.py:11
  375.8 23.5 %copy-start.8 = (s32[1024]{0:T(1024)S(1)}, s32[1024]{0:T(1024)}, u32[]{:S(2)}) copy-start(s32[1024]{0:T(1024)} %param.16) | copy-start | bytes 12292
  417.6 9.3 %copy-start.6 = (pred[128,256]{1,0:T(32,128)(4,1)S(1)}, pred[128,256]{1,0:T(32,128)(4,1)}, u32[]{:S(2)}) copy-start(pred[128,256]{1,0:T(32,128)(4,1)} %constant.45) | copy-start | bytes 98308
  417.6 9.3 %copy-start.4 = (s32[32768]{0:T(1024)S(1)}, s32[32768]{0:T(1024)}, u32[]{:S(2)}) copy-start(s32[32768]{0:T(1024)} %constant.65) | copy-start | bytes 393220
  421.3 159.2 %collective-permute-start = (bf16[128,4096]{1,0:T(8,128)(2,1)}, bf16[128,4096]{1,0:T(8,128)(2,1)}, u32[]{:S(2)}, u32[]{:S(2)}) collective-permute-start(bf16[128,4096]{1,0:T(8,128)(2,1)} %get-tuple-element.11), channel_id=1, source_target_pairs={{0,2},{2,4},{4,6},{6,8},{8,10},{10,12},{12,14},{1,3},{3,5},{5,7},{... | collective-permute-start | bytes 3145736 | tf_op jit(solution)/shard_map/ppermute | solution.py:11
  700.2 9.1 %copy-start = (f32[128,4096]{1,0:T(8,128)S(1)}, f32[128,4096]{1,0:T(8,128)}, u32[]{:S(2)}) copy-start(f32[128,4096]{1,0:T(8,128)} %copy.51) | copy-start | bytes 6291460
  700.2 9.1 %copy-start.1 = (bf16[128,4096]{1,0:T(8,128)(2,1)S(1)}, bf16[128,4096]{1,0:T(8,128)(2,1)}, u32[]{:S(2)}) copy-start(bf16[128,4096]{1,0:T(8,128)(2,1)} %reduce-scatter.2.cloned.1.call-done) | copy-start | bytes 3145732
Sparse Core Ops, SparseCore 0:
  10.1 13.2 all-gather.1
  95.5 148.0 reduce-scatter.1
  709.4 67.4 all-reduce.2
where the time goes:
time: 788 us; the launch traced here: 785 us
  local copies, waits for them, and re-layouts  411 us (52%)
  waiting for transfers between devices  228 us (29%)
  blocking collectives  54.4 us (7%)
  matrix products  51.7 us (7%)
  other arithmetic  19.3 us (2%)
  between operations  13.9 us (2%)
    gather x2, local copies, waits for them, and re-layouts, lag_tables(): jnp.take(filt_vals, np.clip(offsets, 0, tap_count - 1).reshape(-1), axis=1)  259 us
    reduce_scatter x1, waiting for transfers between devices, per_device(): lax.psum_scatter(lax.dot_general(columns, out_weight, (((1,), (1,)), ((),...  147 us
    psum x1, waiting for transfers between devices, per_device(): lax.psum(filt_local.astype(jnp.bfloat16), 'ctx').astype(jnp.float32)  66.4 us
    all_to_all x1, blocking collectives, per_device(): lax.all_to_all(grad_full, 'ctx', split_axis=1, concat_axis=0, tiled=True)  54.4 us
    reshape x2, local copies, waits for them, and re-layouts, lag_tables(): picked = picked.reshape(filt_vals.shape[0], tap_count, 2 * tap_count)  47 us
    reshape x1, local copies, waits for them, and re-layouts, fold_lags(): flat = product.reshape(group_count, 2 * tap_count * tap_count)  35 us
    reshape x1, local copies, waits for them, and re-layouts, fold_lags(): skewed = flat.reshape(group_count, tap_count, 2 * tap_count + 1)  28.3 us
    concatenate x1, local copies, waits for them, and re-layouts, fold_lags(): jnp.concatenate([flat, jnp.zeros((group_count, tap_count), flat.dtype)], 1)  22.4 us
  transfers between devices with their start and end apart: 5, of which 3 were waited for; matrix products, arithmetic and copies ran while one was open for 39% of the time, Pallas kernels for 0%

commit v1 on v0

v1 whole, which is shorter than its diff:
```python
import jax
import jax.numpy as jnp
from jax import lax
from jax.experimental import pallas as pl
from jax.experimental.pallas import tpu as pltpu
from jax.sharding import PartitionSpec as P

BF = jnp.bfloat16
F32 = jnp.float32


def from_behind(array, axis, by):
    length = lax.axis_size(axis)
    pairs = [(i, i + by) for i in range(length) if 0 <= i + by < length]
    return lax.ppermute(array, axis, pairs)


def circulant(row, taps):
    wide = jnp.broadcast_to(row, (taps, taps))
    return pltpu.roll(wide, 0, 1, stride=1, stride_axis=0)


def pick_groups(stacked, taps, chans):
    lanes = lax.broadcasted_iota(jnp.int32, (taps, stacked.shape[1]), 1) // chans
    total = stacked[:taps]
    for i in range(1, stacked.shape[0] // taps):
        total = jnp.where(lanes == i, stacked[i * taps : (i + 1) * taps], total)
    return total


def fill_tables(table_ref, filt_ref, mask_ref, groups, taps):
    for i in range(groups):
        ring = circulant(filt_ref[i : i + 1, :], taps).astype(BF)
        rows = slice(i * taps, (i + 1) * taps)
        table_ref[rows, :taps] = ring * mask_ref[:, :taps]
        table_ref[rows, taps:] = ring * mask_ref[:, taps:]


def forward_kernel(filt_ref, mask_ref, before_ref, mixed_ref, conv_ref, table_ref):
    taps, width = mixed_ref.shape
    groups = filt_ref.shape[0]
    fill_tables(table_ref, filt_ref, mask_ref, groups, taps)
    window = jnp.concatenate([before_ref[...], mixed_ref[...]], 0)
    out = jnp.dot(table_ref[...], window, preferred_element_type=F32)
    conv_ref[...] = pick_groups(out, taps, width // groups)


def backward_kernel(
    filt_ref, back_ref, mask_ref, flip_ref, before_ref, mixed_ref, grad_ref, after_ref, key_ref, value_ref,
    key_out, value_out, filt_out, table_ref, rows_ref,
):
    taps, width = mixed_ref.shape
    groups = filt_ref.shape[0]
    chans = width // groups
    fill_tables(table_ref, filt_ref, back_ref, groups, taps)
    grad = grad_ref[...]
    window = jnp.concatenate([grad, after_ref[...]], 0)
    out = jnp.dot(table_ref[...], window, preferred_element_type=F32)
    total = pick_groups(out, taps, chans)
    key_out[...] = (total * value_ref[...].astype(F32)).astype(BF)
    value_out[...] = (total * key_ref[...].astype(F32)).astype(BF)
    lanes = lax.broadcasted_iota(jnp.int32, (taps, width), 1) // chans
    upturned = jnp.dot(flip_ref[...], grad, preferred_element_type=F32)
    for i in range(groups):
        only = jnp.where(lanes == i, upturned, jnp.zeros_like(upturned))
        rows_ref[i * taps : (i + 1) * taps, :] = only.astype(BF)
    mixed_window = jnp.concatenate([before_ref[...], mixed_ref[...]], 0)
    product = lax.dot_general(
        rows_ref[...], mixed_window, (((1,), (1,)), ((), ())), preferred_element_type=F32
    )
    prev = mask_ref[:, :taps].astype(F32)
    own = mask_ref[:, taps:].astype(F32)
    sums = []
    for i in range(groups):
        block = product[i * taps : (i + 1) * taps]
        folded = block[:, :taps] * prev + block[:, taps:] * own
        turned = pltpu.roll(folded, 0, 1, stride=1, stride_axis=0)
        sums.append(jnp.sum(turned, axis=0, keepdims=True))
    filt_out[...] = jnp.concatenate(sums, 0)


def turn_lanes(array):
    return jnp.roll(jnp.flip(array, 1), 1, axis=1)


def forward_conv(filt_turned, mask, before, mixed, width=128):
    taps, total = mixed.shape
    groups = filt_turned.shape[0] * width // total
    block = pl.BlockSpec((taps, width), lambda i: (0, i))
    return pl.pallas_call(
        forward_kernel,
        grid=(total // width,),
        in_specs=[
            pl.BlockSpec((groups, taps), lambda i: (i, 0)),
            pl.BlockSpec((taps, 2 * taps), lambda i: (0, 0)),
            block,
            block,
        ],
        out_specs=block,
        out_shape=jax.ShapeDtypeStruct((taps, total), F32),
        scratch_shapes=[pltpu.VMEM((groups * taps, 2 * taps), BF)],
        cost_estimate=pl.CostEstimate(
            flops=total * taps * taps * 64, bytes_accessed=total * taps * 8, transcendentals=0
        ),
    )(filt_turned, mask, before, mixed)


def backward_conv(filt, back, mask, before, mixed, grad, after, key, value, width=128):
    taps, total = mixed.shape
    groups = filt.shape[0] * width // total
    block = pl.BlockSpec((taps, width), lambda i: (0, i))
    rows = pl.BlockSpec((groups, taps), lambda i: (i, 0))
    flat = pl.BlockSpec((taps, 2 * taps), lambda i: (0, 0))
    out = jax.ShapeDtypeStruct((taps, total), BF)
    return pl.pallas_call(
        backward_kernel,
        grid=(total // width,),
        in_specs=[rows, flat, flat, pl.BlockSpec((taps, taps), lambda i: (0, 0))] + [block] * 6,
        out_specs=[block, block, rows],
        out_shape=[out, out, jax.ShapeDtypeStruct(filt.shape, F32)],
        scratch_shapes=[
            pltpu.VMEM((groups * taps, 2 * taps), BF),
            pltpu.VMEM((groups * taps, width), BF),
        ],
        cost_estimate=pl.CostEstimate(
            flops=total * taps * taps * 128, bytes_accessed=total * taps * 16, transcendentals=0
        ),
    )(filt, back, mask[::-1], jnp.eye(taps, dtype=BF)[::-1], before, mixed, grad, after, key, value)


def link_masks(genome_ids, first_row, taps):
    pad_ids = jnp.full((taps,), -1, jnp.int32)
    ids_pad = jnp.concatenate([pad_ids, genome_ids, pad_ids])
    ids = lax.dynamic_slice_in_dim(ids_pad, first_row, 3 * taps)
    prev, own, after = ids[:taps], ids[taps : 2 * taps], ids[2 * taps :]
    r = lax.broadcasted_iota(jnp.int32, (taps, taps), 0)
    w = lax.broadcasted_iota(jnp.int32, (taps, taps), 1)
    same = own[:, None] == own[None, :]
    ahead = jnp.concatenate(
        [(own[:, None] == prev[None, :]) & (w > r), same & (w <= r)], 1
    )
    back = jnp.concatenate(
        [same & (w >= r), (own[:, None] == after[None, :]) & (w < r)], 1
    )
    return ahead.astype(BF), back.astype(BF)


def per_device(query_proj, key_proj, value_proj, genome_ids, filters, out_weight, out_grad):
    taps = filters.shape[1]
    row_count = query_proj.shape[0]
    ahead, back = link_masks(genome_ids, lax.axis_index("ctx") * row_count, taps)
    mixed = (key_proj.astype(F32) * value_proj.astype(F32)).astype(BF)
    before = from_behind(mixed, "ctx", 1)
    filt = filters.astype(BF).astype(F32)
    grad_full = lax.all_gather(out_grad, "tp", axis=1, tiled=True)
    columns = lax.all_to_all(grad_full, "ctx", split_axis=1, concat_axis=0, tiled=True)
    dz_vals = lax.psum_scatter(
        lax.dot_general(
            columns, out_weight, (((1,), (1,)), ((), ())), preferred_element_type=F32
        ).astype(BF),
        "ctx",
        scatter_dimension=0,
        tiled=True,
    ).astype(F32)
    conv = forward_conv(turn_lanes(filt), ahead, before, mixed)
    query_grad = (dz_vals * conv).astype(BF)
    grad_conv = (dz_vals * query_proj.astype(F32)).astype(BF)
    after = from_behind(grad_conv, "ctx", -1)
    key_grad, value_grad, turned = backward_conv(
        filt, back, ahead, before, mixed, grad_conv, after, key_proj, value_proj
    )
    filter_grad = jnp.flip(lax.psum(turned.astype(BF), "ctx").astype(F32), 1)
    return (query_grad, key_grad, value_grad, filter_grad)


def solution(mesh):
    rows = P(("group", "ctx"), "tp")
    in_specs = (rows, rows, rows, P("group"), P("tp", None), P("tp", "ctx"), rows)
    out_specs = (rows, rows, rows, P(("group", "tp"), None))
    return jax.shard_map(
        per_device, mesh=mesh, in_specs=in_specs, out_specs=out_specs, check_vma=False
    )
```

time: 788 us -> 401 us (0.51)
  local copies, waits for them, and re-layouts: 411 us -> 10.6 us
  Pallas kernels: 0 us -> 46.5 us
  matrix products: 51.7 us -> 14.8 us
  waiting for transfers between devices: 228 us -> 243 us
  other arithmetic: 19.3 us -> 7.43 us
    gather x2 -> x0, local copies, waits for them, and re-layouts: 259 us -> none  [lag_tables(): jnp.take(filt_vals, np.clip(offsets, 0, tap_count - 1).reshape(-1), axis=1)]
    reshape x6 -> x0, local copies, waits for them, and re-layouts: 115 us -> none  [the longest x2 47 us: lag_tables(): picked = picked.reshape(filt_vals.shape[0], tap_count, 2 * tap_count)]
    ppermute x2, waiting for transfers between devices: 0.01 us -> 53.4 us  [from_behind(): return lax.ppermute(array, axis, pairs)]
    pallas_call x0 -> x2, Pallas kernels: none -> 46.5 us  [the longest x1 25.5 us: backward_conv(): pl.pallas_call(backward_kernel, grid=(total // width,), in_specs=[rows, f...]
    reduce_scatter x1, waiting for transfers between devices: 147 us -> 107 us  [per_device(): lax.psum_scatter(lax.dot_general(columns, out_weight, (((1,), (1,)), ((),...]
    dot_general x3 -> x0, matrix products: 36.9 us -> none  [the longest x1 13.1 us: per_device(): jnp.einsum('tgc,wgc->gtw', grad_rows, window, preferred_element_type=jnp....]
    concatenate x3 -> x0, local copies, waits for them, and re-layouts: 28.2 us -> none  [the longest x1 22.4 us: fold_lags(): jnp.concatenate([flat, jnp.zeros((group_count, tap_count), flat.dtype)], 1)]
    reduce_sum x1 -> x0, other arithmetic: 8.35 us -> none  [fold_lags(): return jnp.flip(jnp.sum(skewed[:, :, 1:tap_count + 1], axis=1), axis=1)]
  transfers between devices with their start and end apart: 5 -> 5, of which waited for: 3 -> 5; matrix products, arithmetic and copies ran while one was open for 39% -> 1% of each run, Pallas kernels for 0% -> 5%
where the time goes in v1:
time: 401 us; the launch traced here: 396 us
  waiting for transfers between devices  243 us (61%)
  blocking collectives  54.4 us (14%)
  Pallas kernels  46.5 us (12%)
  matrix products  14.8 us (4%)
  between operations  13.9 us (3%)
  local copies, waits for them, and re-layouts  10.6 us (3%)
  other arithmetic  7.43 us (2%)
  starting transfers between devices  5.75 us (1%)
    reduce_scatter x1, waiting for transfers between devices, per_device(): lax.psum_scatter(lax.dot_general(columns, out_weight, (((1,), (1,)), ((),...  107 us
    psum x1, waiting for transfers between devices, per_device(): filter_grad = jnp.flip(lax.psum(turned.astype(BF), 'ctx').astype(F32), 1)  68.4 us
    all_to_all x1, blocking collectives, per_device(): lax.all_to_all(grad_full, 'ctx', split_axis=1, concat_axis=0, tiled=True)  54.4 us
    ppermute x2, waiting for transfers between devices, from_behind(): return lax.ppermute(array, axis, pairs)  53.4 us
    pallas_call x1, Pallas kernels, backward_conv(): pl.pallas_call(backward_kernel, grid=(total // width,), in_specs=[rows, f...  25.5 us
    pallas_call x1, Pallas kernels, forward_conv(): pl.pallas_call(forward_kernel, grid=(total // width,), in_specs=[pl.Block...  21 us
    dot_general x1, matrix products, per_device(): lax.dot_general(columns, out_weight, (((1,), (1,)), ((), ())), preferred_...  14.8 us
    all_gather x1, waiting for transfers between devices, per_device(): grad_full = lax.all_gather(out_grad, 'tp', axis=1, tiled=True)  13.9 us
  transfers between devices with their start and end apart: 5, of which 5 were waited for; matrix products, arithmetic and copies ran while one was open for 1% of the time, Pallas kernels for 5%

profile of v1, /device:TPU:0, one launch (start us, length us, event | category | flops | bytes accessed | tf_op | source)
XLA Modules:
  0.0 396.1 jit_solution(5116670320480078764)
XLA Ops:
  7.2 0.0 all-gather.2.cloned.1.call-start
  7.2 2.3 copy.11
  9.5 0.0 all-gather.2.cloned.1.call-update
  9.5 0.0 reduce-scatter.2.cloned.1.call-start
  9.5 13.9 %all-gather.2.cloned.1.call-done = bf16[128,8192]{0,1:T(8,128)(2,1)} async-done(((bf16[128,4096]{0,1:T(8,128)(2,1)}), bf16[128,8192]{0,1:T(8,128)(2,1)}) %all-gather.2.cloned.1.call-update) | async-done | bytes 2097168 | tf_op jit(solution)/shard_map/all_gather | solution.py:155
  23.4 54.4 %all_to_all.19 = bf16[128,8,1024]{0,2,1:T(8,128)(2,1)S(1)} all-to-all(bf16[128,8,1024]{0,2,1:T(8,128)(2,1)} %bitcast.7), channel_id=1, replica_groups=mesh['group'=2,'ctx'=8,'tp'=2] {'ctx'}, dimensions={1} | all-to-all | bytes 4194304 | tf_op jit(solution)/shard_map/all_to_all | solution.py:156
  77.9 2.7 copy.12
  80.5 14.8 %convolution_convert_fusion = bf16[1024,4096]{1,0:T(8,128)(2,1)} fusion(bf16[1024,1024]{1,0:T(8,128)(2,1)} %bitcast.8, bf16[4096,1024]{1,0:T(8,128)(2,1)} %param.12), kind=kOutput, calls=%fused_computation | convolution fusion | flops 8594128896 | bytes 18874368 | tf_op jit(solution)/shard_map/dot_general | solution.py:158
  95.3 0.0 copy-start.1
  95.3 0.0 copy-start.2
  95.3 0.0 reduce-scatter.2.cloned.1.call-update
  95.4 0.0 copy-start.7
  95.4 0.0 copy-start.8
  95.4 0.0 all-reduce.2.cloned.1.call-start
  95.4 1.1 copy-done.1
  96.6 0.3 copy-done.2
  96.9 0.2 multiply_convert_fusion.mixed_ref
  97.1 0.0 copy-start.3
  97.1 4.3 %collective-permute-start = (bf16[128,4096]{1,0:T(8,128)(2,1)S(1)}, bf16[128,4096]{1,0:T(8,128)(2,1)}, u32[]{:S(2)}, u32[]{:S(2)}) collective-permute-start(bf16[128,4096]{1,0:T(8,128)(2,1)S(1)} %multiply_convert_fusion.mixed_ref), channel_id=1, source_target_pairs={{0,2},{2,4},{4,6},{6,8},{8,10},{10,12},{12,14},{1,3},{3,5},{5,7},{... | collective-permute-start | bytes 3145736 | tf_op jit(solution)/shard_map/ppermute | solution.py:15
  101.5 0.0 copy-done.7
  101.5 0.0 copy-start
  101.5 0.1 slice.28
  101.6 0.2 slice.23
  101.8 0.0 copy-done.8
  101.8 0.1 fusion.6
  101.9 0.1 compare_and_fusion
  102.0 0.6 add_convert_fusion.mask_ref
  102.7 0.8 pad_maximum_fusion.filt_ref
  103.4 0.0 copy-start.4
  103.4 29.8 %collective-permute-done.before_ref = bf16[128,4096]{1,0:T(8,128)(2,1)} collective-permute-done((bf16[128,4096]{1,0:T(8,128)(2,1)S(1)}, bf16[128,4096]{1,0:T(8,128)(2,1)}, u32[]{:S(2)}, u32[]{:S(2)}) %collective-permute-start) | collective-permute-done | bytes 1048608 | tf_op jit(solution)/shard_map/ppermute | solution.py:15
  133.2 0.0 copy-done.3
  133.2 21.0 %shard_map.102 = f32[128,4096]{1,0:T(8,128)} custom-call(f32[256,128]{1,0:T(8,128)} %pad_maximum_fusion.filt_ref, bf16[128,256]{1,0:T(8,128)(2,1)} %add_convert_fusion.mask_ref, bf16[128,4096]{1,0:T(8,128)(2,1)} %collective-permute-done.before_ref, bf16[128,4096]{1,0:T(8,128)(2,1)} %copy-done.3), custom_call_target="tpu_custom_call" | custom-call | flops 4294967296 | bytes 4194304 | tf_op jit(solution)/shard_map/pallas_call | solution.py:90
  154.2 0.0 copy-done
  154.2 0.0 copy-start.6
  154.2 107.0 %reduce-scatter.2.cloned.1.call-done = bf16[128,4096]{1,0:T(8,128)(2,1)} async-done(((bf16[1024,4096]{1,0:T(8,128)(2,1)}), bf16[128,4096]{1,0:T(8,128)(2,1)}) %reduce-scatter.2.cloned.1.call-update) | async-done | bytes 1048592 | tf_op jit(solution)/shard_map/reduce_scatter | solution.py:157
  261.3 0.0 copy-done.4
  261.3 3.4 fusion.1
  264.7 0.0 copy-start.5
  264.7 1.3 collective-permute-start.1
  266.0 0.0 copy-done.6
  266.0 0.7 rev.11.mask_ref
  266.7 0.6 rev.12.flip_ref
  267.3 0.6 add_convert_fusion.1.back_ref
  267.9 23.6 %collective-permute-done.1.after_ref = bf16[128,4096]{1,0:T(8,128)(2,1)S(1)} collective-permute-done((bf16[128,4096]{1,0:T(8,128)(2,1)S(1)}, bf16[128,4096]{1,0:T(8,128)(2,1)S(1)}, u32[]{:S(2)}, u32[]{:S(2)}) %collective-permute-start.1) | collective-permute-done | bytes 1048608 | tf_op jit(solution)/shard_map/ppermute | solution.py:15
  291.5 0.0 copy-done.5
  291.5 0.0 copy-start.9
  291.5 1.0 copy-done.9
  292.5 25.5 %shard_map.103 = (bf16[128,4096]{1,0:T(8,128)(2,1)}, bf16[128,4096]{1,0:T(8,128)(2,1)}, f32[256,128]{1,0:T(8,128)}) custom-call(f32[256,128]{1,0:T(8,128)} %copy-done, bf16[128,256]{1,0:T(8,128)(2,1)} %add_convert_fusion.1.back_ref, bf16[128,256]{1,0:T(8,128)(2,1)} %rev.11.mask_ref, bf16[128,128]{1,0:T(8,128)(2,1)} %rev.12.flip_ref, ...), custom_call_target="tpu_custom_call" | custom-call | flops 8589934592 | bytes 8388608 | tf_op jit(solution)/shard_map/pallas_call | solution.py:115
  318.0 1.5 convert_element_type.58
  319.5 0.0 all-reduce.2.cloned.1.call-update
  319.6 68.4 %all-reduce.2.cloned.1.call-done = bf16[256,128]{1,0:T(8,128)(2,1)} async-done(((bf16[256,128]{1,0:T(8,128)(2,1)}), bf16[256,128]{1,0:T(8,128)(2,1)}) %all-reduce.2.cloned.1.call-update) | async-done | bytes 65552 | tf_op jit(solution)/shard_map/psum | solution.py:172
  388.0 1.6 rev.13
  (4 shorter events, 0.0 us)
Async XLA Ops:
  7.2 16.3 %all-gather.2.cloned.1.call-start = ((), (), s32[]{:S(2)}) async-start(), calls=%async_computation.2 | async-start | bytes 3145728 | tf_op jit(solution)/shard_map/all_gather | solution.py:155
  9.5 251.8 %reduce-scatter.2.cloned.1.call-start = ((), (), s32[]{:S(2)}) async-start(), calls=%async_computation.3 | async-start | bytes 9437184 | tf_op jit(solution)/shard_map/reduce_scatter | solution.py:157
  95.3 1.2 copy-start.1
  95.3 1.5 copy-start.2
  95.4 6.1 %copy-start.7 = (f32[256,128]{1,0:T(8,128)S(1)}, f32[256,128]{1,0:T(8,128)}, u32[]{:S(2)}) copy-start(f32[256,128]{1,0:T(8,128)} %param.11) | copy-start | bytes 393220
  95.4 6.4 %copy-start.8 = (s32[1024]{0:T(1024)S(1)}, s32[1024]{0:T(1024)}, u32[]{:S(2)}) copy-start(s32[1024]{0:T(1024)} %param.10) | copy-start | bytes 12292
  95.4 292.6 %all-reduce.2.cloned.1.call-start = ((), (), s32[]{:S(2)}) async-start(), calls=%async_computation.4 | async-start | bytes 131072 | tf_op jit(solution)/shard_map/psum | solution.py:172
  97.1 36.1 %copy-start.3 = (bf16[128,4096]{1,0:T(8,128)(2,1)}, bf16[128,4096]{1,0:T(8,128)(2,1)S(1)}, u32[]{:S(2)}) copy-start(bf16[128,4096]{1,0:T(8,128)(2,1)S(1)} %multiply_convert_fusion.mixed_ref) | copy-start | bytes 3145732
  97.1 36.1 %collective-permute-start = (bf16[128,4096]{1,0:T(8,128)(2,1)S(1)}, bf16[128,4096]{1,0:T(8,128)(2,1)}, u32[]{:S(2)}, u32[]{:S(2)}) collective-permute-start(bf16[128,4096]{1,0:T(8,128)(2,1)S(1)} %multiply_convert_fusion.mixed_ref), channel_id=1, source_target_pairs={{0,2},{2,4},{4,6},{6,8},{8,10},{10,12},{12,14},{1,3},{3,5},{5,7},{... | collective-permute-start | bytes 3145736 | tf_op jit(solution)/shard_map/ppermute | solution.py:15
  101.5 52.7 %copy-start = (f32[256,128]{1,0:T(8,128)}, f32[256,128]{1,0:T(8,128)S(1)}, u32[]{:S(2)}) copy-start(f32[256,128]{1,0:T(8,128)S(1)} %convert_convert_fusion.filt_ref) | copy-start | bytes 393220
  103.4 157.8 %copy-start.4 = (bf16[128,4096]{1,0:T(8,128)(2,1)S(1)}, bf16[128,4096]{1,0:T(8,128)(2,1)}, u32[]{:S(2)}) copy-start(bf16[128,4096]{1,0:T(8,128)(2,1)} %param.7) | copy-start | bytes 3145732
  154.2 111.7 %copy-start.6 = (bf16[128,256]{1,0:T(8,128)(2,1)S(1)}, bf16[128,256]{1,0:T(8,128)(2,1)}, u32[]{:S(2)}) copy-start(bf16[128,256]{1,0:T(8,128)(2,1)} %add_convert_fusion.mask_ref) | copy-start | bytes 196612
  264.7 26.9 %copy-start.5 = (bf16[128,4096]{1,0:T(8,128)(2,1)}, bf16[128,4096]{1,0:T(8,128)(2,1)S(1)}, u32[]{:S(2)}) copy-start(bf16[128,4096]{1,0:T(8,128)(2,1)S(1)} %get-tuple-element.10.grad_ref) | copy-start | bytes 3145732
  264.7 26.9 %collective-permute-start.1 = (bf16[128,4096]{1,0:T(8,128)(2,1)S(1)}, bf16[128,4096]{1,0:T(8,128)(2,1)S(1)}, u32[]{:S(2)}, u32[]{:S(2)}) collective-permute-start(bf16[128,4096]{1,0:T(8,128)(2,1)S(1)} %get-tuple-element.10.grad_ref), channel_id=1, source_target_pairs={{2,0},{4,2},{6,4},{8,6},{10,8},{12,10},{14,12},{3,1},{5,3},{7,5},{... | collective-permute-start | bytes 3145736 | tf_op jit(solution)/shard_map/ppermute | solution.py:15
  291.5 1.0 copy-start.9
Sparse Core Ops, SparseCore 0:
  10.1 13.2 all-gather.1
  95.5 165.7 reduce-scatter.1
  319.7 68.2 all-reduce.1

commit v2 on v1

v2 whole, which is shorter than its diff:
```python
import functools
import jax
import jax.numpy as jnp
from jax import lax
from jax.experimental import pallas as pl
from jax.experimental.pallas import tpu as pltpu
from jax.sharding import PartitionSpec as P

BF = jnp.bfloat16
F32 = jnp.float32


def circulant(row, taps):
    wide = jnp.broadcast_to(row, (taps, taps))
    return pltpu.roll(wide, 0, 1, stride=1, stride_axis=0)


def pick_groups(stacked, taps, chans):
    lanes = lax.broadcasted_iota(jnp.int32, (taps, stacked.shape[1]), 1) // chans
    total = stacked[:taps]
    for i in range(1, stacked.shape[0] // taps):
        total = jnp.where(lanes == i, stacked[i * taps : (i + 1) * taps], total)
    return total


def fill_tables(table_ref, filt_ref, mask_ref, groups, taps):
    for i in range(groups):
        ring = circulant(filt_ref[i : i + 1, :], taps).astype(BF)
        rows = slice(i * taps, (i + 1) * taps)
        table_ref[rows, :taps] = ring * mask_ref[:, :taps]
        table_ref[rows, taps:] = ring * mask_ref[:, taps:]


def link_masks(genome_ids, first_row, taps):
    pad_ids = jnp.full((taps,), -1, jnp.int32)
    ids_pad = jnp.concatenate([pad_ids, genome_ids, pad_ids])
    ids = lax.dynamic_slice_in_dim(ids_pad, first_row, 3 * taps)
    prev, own, after = ids[:taps], ids[taps : 2 * taps], ids[2 * taps :]
    r = lax.broadcasted_iota(jnp.int32, (taps, taps), 0)
    w = lax.broadcasted_iota(jnp.int32, (taps, taps), 1)
    same = own[:, None] == own[None, :]
    ahead = jnp.concatenate(
        [(own[:, None] == prev[None, :]) & (w > r), same & (w <= r)], 1
    )
    back = jnp.concatenate(
        [same & (w >= r), (own[:, None] == after[None, :]) & (w < r)], 1
    )
    return ahead.astype(BF), back.astype(BF)


STREAMS = 4
BLOCK = 128
MESH = pl.DeviceIdType.MESH


def turn_lanes(array):
    return jnp.roll(jnp.flip(array, 1), 1, axis=1)


def ring_to_ctx(place, n):
    late = place // (n // 2)
    return (1 - late) * (2 * place) + late * (2 * (n - 1 - place) + 1)


def ctx_to_ring(ctx, n):
    odd = ctx % 2
    return (1 - odd) * (ctx // 2) + odd * (n - 1 - ctx // 2)


def step_kernel(
    n, turned_ref, filt_ref, ahead_ref, back_ref, upside_ref, flip_ref,
    query_hbm, key_hbm, value_hbm, weight_hbm, grad_hbm,
    query_out, key_out, value_out, filt_out,
    query_ref, key_ref, value_ref, weight_ref, cols_ref, ring_ref, part_ref,
    window_ref, gwin_ref, conv_ref, table_ref, rows_ref, fpart_ref, fin_ref,
    local_sem, a2a_send, a2a_recv, pass_send, pass_recv, own_send,
    ring_send, ring_recv, mixed_sem, halo_send, halo_recv,
    fold_send, fold_recv, share_send, share_recv,
):
    taps, total = query_ref.shape
    width = weight_ref.shape[1]
    held = grad_hbm.shape[1] // width
    chunk = total // STREAMS
    blocks = total // BLOCK
    groups = filt_ref.shape[0] // blocks
    chans = BLOCK // groups
    me = lax.axis_index("ctx")
    core = lax.axis_index("tp")
    place = ctx_to_ring(me, n)
    half_rows = taps // 2
    mine = filt_ref.shape[0] // n

    def remote(src, dst, send, recv, ctx, tp):
        return pltpu.make_async_remote_copy(
            src_ref=src, dst_ref=dst, send_sem=send, recv_sem=recv,
            device_id={"ctx": ctx, "tp": tp}, device_id_type=MESH,
        )

    loads = [
        pltpu.make_async_copy(src, dst, local_sem.at[i])
        for i, (src, dst) in enumerate([
            (key_hbm, key_ref), (value_hbm, value_ref), (weight_hbm, weight_ref),
            (query_hbm, query_ref),
        ])
    ]
    for load in loads:
        load.start()

    barrier = pltpu.get_barrier_semaphore()
    for gap in range(n):
        for other in range(2):
            if gap or other:
                pl.semaphore_signal(
                    barrier, inc=1,
                    device_id={"ctx": (me + gap) % n, "tp": (core + other) % 2},
                    device_id_type=MESH,
                )
    pl.semaphore_wait(barrier, 2 * n - 1)

    def at_gap(gap):
        return ring_to_ctx((place + gap + n) % n, n)

    def columns_of(ctx):
        return pl.ds(pl.multiple_of((ctx % held) * width, width), width)

    def send_block(gap, half):
        ctx = at_gap(gap)
        rows = pl.ds(half * half_rows, half_rows)
        return ctx, remote(
            grad_hbm.at[rows, columns_of(ctx)], cols_ref.at[me, rows, :],
            a2a_send.at[gap % n, half], a2a_recv.at[me], ctx, half,
        )

    gaps = []
    for d in range(1, n // 2 + 1):
        gaps += [d, -d] if d < n // 2 else [d]

    def each_send(act):
        for gap in gaps:
            @pl.when(at_gap(gap) // held == core)
            def _(gap=gap):
                for half in range(2):
                    act(send_block(gap, half)[1])

    own_local = pltpu.make_async_copy(
        grad_hbm.at[:, columns_of(me)], cols_ref.at[me], local_sem.at[4]
    )
    own_remote = remote(
        grad_hbm.at[:, columns_of(me)], cols_ref.at[me],
        own_send, pass_recv.at[me], me, 1 - core,
    )
    each_send(lambda copy: copy.start())

    @pl.when(me // held == core)
    def _():
        own_local.start()
        own_remote.start()

    loads[0].wait()
    loads[1].wait()
    window_ref[taps:, :] = (
        key_ref[...].astype(F32) * value_ref[...].astype(F32)
    ).astype(BF)
    mixed_copy = remote(
        window_ref.at[pl.ds(taps, taps), :], window_ref.at[pl.ds(0, taps), :],
        mixed_sem.at[0], mixed_sem.at[1], (me + 1) % n, core,
    )

    @pl.when(me < n - 1)
    def _():
        mixed_copy.start()

    @pl.when(me == 0)
    def _():
        window_ref[:taps, :] = jnp.zeros((taps, total), BF)

    def passing(ctx, half):
        rows = pl.ds(pl.multiple_of(half * half_rows, half_rows), half_rows)
        spot = cols_ref.at[ctx, rows, :]
        return remote(spot, spot, pass_send.at[ctx], pass_recv.at[ctx], me, 1 - core)

    def arrived(ctx):
        rows = pl.ds(pl.multiple_of(core * half_rows, half_rows), half_rows)
        spot = cols_ref.at[ctx, rows, :]
        remote(spot, spot, pass_send.at[ctx], a2a_recv.at[ctx], me, 1 - core).wait_recv()

    def pass_on(d):
        def one(gap):
            ctx = at_gap(gap)
            arrived(ctx)
            passing(ctx, core).start()

        one(-1 - d)

        @pl.when(d < n // 2 - 1)
        def _():
            one(1 + d)

    def passed(d):
        passing(at_gap(-1 - d), 1 - core).wait_recv()

        @pl.when(d < n // 2 - 1)
        def _():
            passing(at_gap(1 + d), 1 - core).wait_recv()

    def block_lanes(i):
        return pl.ds(pl.multiple_of(i * BLOCK, BLOCK), BLOCK)

    def block_groups(i):
        return pl.ds(pl.multiple_of(i * groups, groups), groups)

    def conv_block(i):
        fill_tables(table_ref, turned_ref[block_groups(i), :], ahead_ref, groups, taps)
        out = jnp.dot(
            table_ref[...], window_ref[:, block_lanes(i)], preferred_element_type=F32
        )
        conv_ref[:, block_lanes(i)] = pick_groups(out, taps, chans)

    def ring_copy(k, step):
        gap = 1 if k % 2 == 0 else -1
        return remote(
            ring_ref.at[k, step], ring_ref.at[k, step + 1],
            ring_send.at[k, step], ring_recv.at[k, step + 1], at_gap(gap), core,
        )

    def ring_arrival(k, step):
        gap = 1 if k % 2 == 0 else -1
        return remote(
            ring_ref.at[k, step], ring_ref.at[k, step],
            ring_send.at[k, step], ring_recv.at[k, step], at_gap(gap), core,
        )

    def multiply(k, step):
        gap = -1 - step if k % 2 == 0 else 1 + step
        rows = cols_ref[ring_to_ctx((place + gap + 2 * n) % n, n)]
        part_ref[...] = lax.dot_general(
            rows, weight_ref[pl.ds(k * chunk, chunk), :], (((1,), (1,)), ((), ())),
            preferred_element_type=F32,
        ).astype(BF)

    pass_on(0)
    loads[2].wait()
    slots = (n - 2) * STREAMS

    def ring_step(step, carry):
        @pl.when(step < n // 2)
        def _():
            passed(step)

        @pl.when((step == 1) & (me > 0))
        def _():
            mixed_copy.wait_recv()

        for k in range(STREAMS):
            multiply(k, step)

            @pl.when(step == 0)
            def _(k=k):
                ring_ref[k, step] = part_ref[...]

            @pl.when(step > 0)
            def _(k=k):
                ring_arrival(k, step).wait_recv()
                ring_ref[k, step] = (
                    ring_ref[k, step].astype(F32) + part_ref[...].astype(F32)
                ).astype(BF)

            ring_copy(k, step).start()

            @pl.when(step > 0)
            def _(k=k):
                slot = (step - 1) * STREAMS + k
                lax.fori_loop(
                    slot * blocks // slots, (slot + 1) * blocks // slots,
                    lambda i, c: (conv_block(i), c)[1], 0,
                )

        @pl.when(step + 1 < n // 2)
        def _():
            pass_on(step + 1)

        return carry

    lax.fori_loop(0, n - 1, ring_step, 0)

    @pl.when(me // held == core)
    def _():
        own_local.wait()
        own_remote.wait_send()

    @pl.when(me // held != core)
    def _():
        own_remote.wait_recv()

    loads[3].wait()

    @pl.when(me == n - 1)
    def _():
        gwin_ref[taps:, :] = jnp.zeros((taps, total), BF)

    def halo_copy(k):
        cols = pl.ds(k * chunk, chunk)
        return remote(
            gwin_ref.at[pl.ds(0, taps), cols], gwin_ref.at[pl.ds(taps, taps), cols],
            halo_send.at[k], halo_recv.at[k], (me + n - 1) % n, core,
        )

    for k in range(STREAMS):
        cols = pl.ds(k * chunk, chunk)
        multiply(k, n - 1)
        ring_arrival(k, n - 1).wait_recv()
        dz = ring_ref[k, n - 1].astype(F32) + part_ref[...].astype(F32)
        dz = dz.astype(BF).astype(F32)
        gwin_ref[:taps, cols] = (dz * query_ref[:, cols].astype(F32)).astype(BF)

        @pl.when(me > 0)
        def _(k=k):
            halo_copy(k).start()

        query_out[:, cols] = (dz * conv_ref[:, cols]).astype(BF)

    prev = upside_ref[:, :taps].astype(F32)
    own = upside_ref[:, taps:].astype(F32)
    lanes = lax.broadcasted_iota(jnp.int32, (taps, BLOCK), 1) // chans

    def filter_block(i, carry):
        upturned = jnp.dot(
            flip_ref[...], gwin_ref[:taps, block_lanes(i)], preferred_element_type=F32
        )
        for g in range(groups):
            only = jnp.where(lanes == g, upturned, jnp.zeros_like(upturned))
            rows_ref[g * taps : (g + 1) * taps, :] = only.astype(BF)
        product = lax.dot_general(
            rows_ref[...], window_ref[:, block_lanes(i)], (((1,), (1,)), ((), ())),
            preferred_element_type=F32,
        )
        sums = []
        for g in range(groups):
            block = product[g * taps : (g + 1) * taps]
            folded = block[:, :taps] * prev + block[:, taps:] * own
            moved = pltpu.roll(folded, 0, 1, stride=1, stride_axis=0)
            sums.append(jnp.sum(moved, axis=0, keepdims=True))
        fpart_ref[block_groups(i), :] = jnp.concatenate(sums, 0)
        return carry

    lax.fori_loop(0, blocks, filter_block, 0)

    def slice_of(ctx):
        return pl.ds(pl.multiple_of(ctx * mine, mine), mine)

    def fold_copy(gap):
        ctx = (me + gap) % n
        return remote(
            fpart_ref.at[slice_of(ctx), :], fin_ref.at[gap],
            fold_send.at[gap], fold_recv.at[gap], ctx, core,
        )

    def share_copy(gap):
        return remote(
            filt_out.at[slice_of(me), :], filt_out.at[slice_of(me), :],
            share_send.at[gap], share_recv.at[gap], (me + gap) % n, core,
        )

    for gap in range(1, n):
        fold_copy(gap).start()

    def backward_block(i, carry):
        fill_tables(table_ref, filt_ref[block_groups(i), :], back_ref, groups, taps)
        out = jnp.dot(
            table_ref[...], gwin_ref[:, block_lanes(i)], preferred_element_type=F32
        )
        grad = pick_groups(out, taps, chans)
        cols = block_lanes(i)
        key_out[:, cols] = (grad * value_ref[:, cols].astype(F32)).astype(BF)
        value_out[:, cols] = (grad * key_ref[:, cols].astype(F32)).astype(BF)
        return carry

    for k in range(STREAMS):
        @pl.when(me < n - 1)
        def _(k=k):
            halo_copy(k).wait_recv()

        lax.fori_loop(k * blocks // STREAMS, (k + 1) * blocks // STREAMS, backward_block, 0)
        if k == STREAMS - 2:
            summed = fpart_ref[slice_of(me), :]
            for gap in range(1, n):
                fold_copy(gap).wait_recv()
                summed = summed + fin_ref[gap]
            filt_out[slice_of(me), :] = summed
            for gap in range(1, n):
                share_copy(gap).start()

    for gap in range(1, n):
        sender = (me + n - gap) % n
        remote(
            filt_out.at[slice_of(sender), :], filt_out.at[slice_of(sender), :],
            share_send.at[gap], share_recv.at[gap], sender, core,
        ).wait_recv()

    each_send(lambda copy: copy.wait_send())
    for gap in gaps:
        passing(at_gap(gap), core).wait_send()

    @pl.when(me < n - 1)
    def _():
        mixed_copy.wait_send()

    for k in range(STREAMS):
        for step in range(n - 1):
            ring_copy(k, step).wait_send()

        @pl.when(me > 0)
        def _(k=k):
            halo_copy(k).wait_send()

    for gap in range(1, n):
        fold_copy(gap).wait_send()
        share_copy(gap).wait_send()


def per_device(query_proj, key_proj, value_proj, genome_ids, filters, out_weight, out_grad):
    taps = filters.shape[1]
    n = lax.axis_size("ctx")
    row_count, total = query_proj.shape
    width = out_weight.shape[1]
    groups = filters.shape[0] * BLOCK // total
    ahead, back = link_masks(genome_ids, lax.axis_index("ctx") * row_count, taps)
    filt = filters.astype(BF).astype(F32)
    out = jax.ShapeDtypeStruct((row_count, total), BF)
    vmem = pl.BlockSpec(memory_space=pltpu.VMEM)
    anywhere = pl.BlockSpec(memory_space=pl.ANY)
    dma = pltpu.SemaphoreType.DMA
    query_grad, key_grad, value_grad, filter_grad = pl.pallas_call(
        functools.partial(step_kernel, n),
        in_specs=[vmem] * 6 + [anywhere] * 5,
        out_specs=[vmem] * 4,
        out_shape=[out, out, out, jax.ShapeDtypeStruct(filt.shape, F32)],
        scratch_shapes=[
            pltpu.VMEM((row_count, total), BF),
            pltpu.VMEM((row_count, total), BF),
            pltpu.VMEM((row_count, total), BF),
            pltpu.VMEM(out_weight.shape, BF),
            pltpu.VMEM((n, row_count, width), BF),
            pltpu.VMEM((STREAMS, n, row_count, total // STREAMS), BF),
            pltpu.VMEM((row_count, total // STREAMS), BF),
            pltpu.VMEM((2 * taps, total), BF),
            pltpu.VMEM((2 * taps, total), BF),
            pltpu.VMEM((row_count, total), F32),
            pltpu.VMEM((groups * taps, 2 * taps), BF),
            pltpu.VMEM((groups * taps, BLOCK), BF),
            pltpu.VMEM(filt.shape, F32),
            pltpu.VMEM((n, filt.shape[0] // n, taps), F32),
            dma((5,)), dma((n, 2)), dma((n,)), dma((n,)), dma((n,)), dma,
            dma((STREAMS, n)), dma((STREAMS, n)), dma((2,)), dma((STREAMS,)), dma((STREAMS,)),
            dma((n,)), dma((n,)), dma((n,)), dma((n,)),
        ],
        compiler_params=pltpu.CompilerParams(
            collective_id=0, has_side_effects=True, vmem_limit_bytes=56 * 1024 * 1024
        ),
    )(
        turn_lanes(filt), filt, ahead, back, ahead[::-1], jnp.eye(taps, dtype=BF)[::-1],
        query_proj, key_proj, value_proj, out_weight, out_grad,
    )
    return (query_grad, key_grad, value_grad, jnp.flip(filter_grad, 1))


def solution(mesh):
    rows = P(("group", "ctx"), "tp")
    in_specs = (rows, rows, rows, P("group"), P("tp", None), P("tp", "ctx"), rows)
    out_specs = (rows, rows, rows, P(("group", "tp"), None))
    return jax.shard_map(
        per_device, mesh=mesh, in_specs=in_specs, out_specs=out_specs, check_vma=False
    )
```

time: 401 us -> 181 us (0.45); the launches traced: 396 us -> 181 us
  waiting for transfers between devices: 243 us -> 0 us
  Pallas kernels: 46.5 us -> 166 us
  blocking collectives: 54.4 us -> 0 us
  matrix products: 14.8 us -> 0 us
  between operations: 13.9 us -> 0.69 us
  starting transfers between devices: 5.75 us -> 0 us
  other arithmetic: 7.43 us -> 3.24 us
    pallas_call x2 -> x1, Pallas kernels: 46.5 us -> 166 us  [per_device(): pl.pallas_call(functools.partial(step_kernel, n), in_specs=[vmem] * 6 + [...]
    reduce_scatter x1 -> x0, waiting for transfers between devices: 107 us -> none  [per_device(): lax.psum_scatter(lax.dot_general(columns, out_weight, (((1,), (1,)), ((),...]
    psum x1 -> x0, waiting for transfers between devices: 68.4 us -> none  [per_device(): filter_grad = jnp.flip(lax.psum(turned.astype(BF), 'ctx').astype(F32), 1)]
    all_to_all x1 -> x0, blocking collectives: 54.4 us -> none  [per_device(): lax.all_to_all(grad_full, 'ctx', split_axis=1, concat_axis=0, tiled=True)]
    ppermute x2 -> x0, waiting for transfers between devices: 53.4 us -> none  [from_behind(): return lax.ppermute(array, axis, pairs)]
    dot_general x1 -> x0, matrix products: 14.8 us -> none  [per_device(): lax.dot_general(columns, out_weight, (((1,), (1,)), ((), ())), preferred_...]
    all_gather x1 -> x0, waiting for transfers between devices: 13.9 us -> none  [per_device(): grad_full = lax.all_gather(out_grad, 'tp', axis=1, tiled=True)]
    ppermute x2 -> x0, starting transfers between devices: 5.63 us -> none  [from_behind(): return lax.ppermute(array, axis, pairs)]
  transfers between devices with their start and end apart: 5 -> 0, of which waited for: 5 -> 0; matrix products, arithmetic and copies ran while one was open for 1% -> 0% of each run, Pallas kernels for 5% -> 0%
where the time goes in v2:
time: 181 us
  Pallas kernels  166 us (92%)
  local copies, waits for them, and re-layouts  10.1 us (6%)
  other arithmetic  3.24 us (2%)
    pallas_call x1, Pallas kernels, per_device(): pl.pallas_call(functools.partial(step_kernel, n), in_specs=[vmem] * 6 + [...  166 us
    unnamed x7, local copies, waits for them, and re-layouts  6.87 us

profile of v2, /device:TPU:0, one launch (start us, length us, event | category | flops | bytes accessed | tf_op | source)
XLA Modules:
  0.0 180.5 jit_solution(10656930033943117210)
XLA Ops:
  0.6 0.8 fusion.4
  1.4 0.6 rev.12.flip_ref
  2.1 0.1 compare_and_fusion
  2.2 0.7 add_convert_fusion
  2.8 0.0 copy-start.1
  2.8 0.7 rev.11.upside_ref
  3.5 0.9 convert_convert_fusion.filt_ref
  4.4 0.0 copy-start
  4.5 0.1 slice.28
  4.6 0.2 slice.23
  4.7 0.8 pad_maximum_fusion.turned_ref
  5.5 0.0 copy-done.1
  5.5 0.0 copy-done
  5.5 166.5 %shard_map.102 = (bf16[128,4096]{1,0:T(8,128)(2,1)}, bf16[128,4096]{1,0:T(8,128)(2,1)}, bf16[128,4096]{1,0:T(8,128)(2,1)}, f32[256,128]{1,0:T(8,128)}) custom-call(f32[256,128]{1,0:T(8,128)} %pad_maximum_fusion.turned_ref, f32[256,128]{1,0:T(8,128)} %copy-done, bf16[128,256]{1,0:T(8,128)(2,1)} %copy-done.1, bf16[128,256]{1,0:T(8,128)(2,1)} %get-tuple-element.20.back_ref, ...), custom_call_target="tpu_custom_call" | custom-call | tf_op jit(solution)/shard_map/pallas_call | solution.py:433
  172.0 1.6 rev.13
  173.6 2.3 %copy.14 = bf16[128,4096]{1,0:T(8,128)(2,1)} copy(bf16[128,4096]{1,0:T(8,128)(2,1)} %get-tuple-element.25) | data formatting | bytes 2097152
  175.9 2.3 %copy.15 = bf16[128,4096]{1,0:T(8,128)(2,1)} copy(bf16[128,4096]{1,0:T(8,128)(2,1)} %get-tuple-element.26) | data formatting | bytes 2097152
  178.2 2.3 %copy.16 = bf16[128,4096]{1,0:T(8,128)(2,1)} copy(bf16[128,4096]{1,0:T(8,128)(2,1)} %get-tuple-element.27) | data formatting | bytes 2097152
  (3 shorter events, 0.0 us)
Async XLA Ops:
  2.8 2.7 %copy-start.1 = (bf16[128,256]{1,0:T(8,128)(2,1)}, bf16[128,256]{1,0:T(8,128)(2,1)S(1)}, u32[]{:S(2)}) copy-start(bf16[128,256]{1,0:T(8,128)(2,1)S(1)} %get-tuple-element.19.ahead_ref) | copy-start | bytes 196612
  4.4 1.1 copy-start

commit v3 on v2

--- a/solution.py
+++ b/solution.py
@@ -68,11 +68,11 @@
 
 
 def step_kernel(
-    n, turned_ref, filt_ref, ahead_ref, back_ref, upside_ref, flip_ref,
+    n, turned_ref, filt_ref, ahead_ref, back_ref,
     query_hbm, key_hbm, value_hbm, weight_hbm, grad_hbm,
     query_out, key_out, value_out, filt_out,
     query_ref, key_ref, value_ref, weight_ref, cols_ref, ring_ref, part_ref,
-    window_ref, gwin_ref, conv_ref, table_ref, rows_ref, fpart_ref, fin_ref,
+    window_ref, gwin_ref, conv_ref, table_ref, tables_ref, rows_ref, fpart_ref, fin_ref,
     local_sem, a2a_send, a2a_recv, pass_send, pass_recv, own_send,
     ring_send, ring_recv, mixed_sem, halo_send, halo_recv,
     fold_send, fold_recv, share_send, share_recv,
@@ -216,6 +216,11 @@
         )
         conv_ref[:, block_lanes(i)] = pick_groups(out, taps, chans)
 
+    def back_table(i):
+        fill_tables(
+            tables_ref.at[i], filt_ref[block_groups(i), :], back_ref, groups, taps
+        )
+
     def ring_copy(k, step):
         gap = 1 if k % 2 == 0 else -1
         return remote(
@@ -241,6 +246,7 @@
     pass_on(0)
     loads[2].wait()
     slots = (n - 2) * STREAMS
+    turns = (n - 1) * STREAMS
 
     def ring_step(step, carry):
         @pl.when(step < n // 2)
@@ -266,6 +272,11 @@
                 ).astype(BF)
 
             ring_copy(k, step).start()
+            turn = step * STREAMS + k
+            lax.fori_loop(
+                turn * blocks // turns, (turn + 1) * blocks // turns,
+                lambda i, c: (back_table(i), c)[1], 0,
+            )
 
             @pl.when(step > 0)
             def _(k=k):
@@ -319,13 +330,17 @@
 
         query_out[:, cols] = (dz * conv_ref[:, cols]).astype(BF)
 
-    prev = upside_ref[:, :taps].astype(F32)
-    own = upside_ref[:, taps:].astype(F32)
+    down = lax.broadcasted_iota(jnp.int32, (taps, taps), 0)
+    across = lax.broadcasted_iota(jnp.int32, (taps, taps), 1)
+    flip = jnp.where(down + across == taps - 1, 1.0, 0.0).astype(BF)
+    upside = jnp.dot(flip, ahead_ref[...], preferred_element_type=F32)
+    prev = upside[:, :taps]
+    own = upside[:, taps:]
     lanes = lax.broadcasted_iota(jnp.int32, (taps, BLOCK), 1) // chans
 
     def filter_block(i, carry):
         upturned = jnp.dot(
-            flip_ref[...], gwin_ref[:taps, block_lanes(i)], preferred_element_type=F32
+            flip, gwin_ref[:taps, block_lanes(i)], preferred_element_type=F32
         )
         for g in range(groups):
             only = jnp.where(lanes == g, upturned, jnp.zeros_like(upturned))
@@ -365,9 +380,8 @@
         fold_copy(gap).start()
 
     def backward_block(i, carry):
-        fill_tables(table_ref, filt_ref[block_groups(i), :], back_ref, groups, taps)
         out = jnp.dot(
-            table_ref[...], gwin_ref[:, block_lanes(i)], preferred_element_type=F32
+            tables_ref[i], gwin_ref[:, block_lanes(i)], preferred_element_type=F32
         )
         grad = pick_groups(out, taps, chans)
         cols = block_lanes(i)
@@ -432,7 +446,7 @@
     dma = pltpu.SemaphoreType.DMA
     query_grad, key_grad, value_grad, filter_grad = pl.pallas_call(
         functools.partial(step_kernel, n),
-        in_specs=[vmem] * 6 + [anywhere] * 5,
+        in_specs=[vmem] * 4 + [anywhere] * 5,
         out_specs=[vmem] * 4,
         out_shape=[out, out, out, jax.ShapeDtypeStruct(filt.shape, F32)],
         scratch_shapes=[
@@ -447,6 +461,7 @@
             pltpu.VMEM((2 * taps, total), BF),
             pltpu.VMEM((row_count, total), F32),
             pltpu.VMEM((groups * taps, 2 * taps), BF),
+            pltpu.VMEM((total // BLOCK, groups * taps, 2 * taps), BF),
             pltpu.VMEM((groups * taps, BLOCK), BF),
             pltpu.VMEM(filt.shape, F32),
             pltpu.VMEM((n, filt.shape[0] // n, taps), F32),
@@ -455,10 +470,10 @@
             dma((n,)), dma((n,)), dma((n,)), dma((n,)),
         ],
         compiler_params=pltpu.CompilerParams(
-            collective_id=0, has_side_effects=True, vmem_limit_bytes=56 * 1024 * 1024
+            collective_id=0, has_side_effects=True, vmem_limit_bytes=60 * 1024 * 1024
         ),
     )(
-        turn_lanes(filt), filt, ahead, back, ahead[::-1], jnp.eye(taps, dtype=BF)[::-1],
+        turn_lanes(filt), filt, ahead, back,
         query_proj, key_proj, value_proj, out_weight, out_grad,
     )
     return (query_grad, key_grad, value_grad, jnp.flip(filter_grad, 1))

time: 181 us -> 180 us (level)
    unnamed x7 -> x5, local copies, waits for them, and re-layouts: 6.87 us -> 6.87 us
where the time goes in v3:
time: 180 us; the launch traced here: 179 us
  Pallas kernels  166 us (92%)
  local copies, waits for them, and re-layouts  8.79 us (5%)
  other arithmetic  3.25 us (2%)
    pallas_call x1, Pallas kernels, per_device(): pl.pallas_call(functools.partial(step_kernel, n), in_specs=[vmem] * 4 + [...  166 us
    unnamed x5, local copies, waits for them, and re-layouts  6.87 us

profile of v3, /device:TPU:0, one launch (start us, length us, event | category | flops | bytes accessed | tf_op | source)
XLA Modules:
  0.0 179.2 jit_solution(14534708977321416298)
XLA Ops:
  0.6 0.8 fusion.3
  1.4 0.1 compare_and_fusion
  1.5 0.7 add_convert_fusion
  2.2 0.9 convert_convert_fusion.filt_ref
  3.1 0.0 copy-start
  3.1 0.1 slice.28
  3.2 0.2 slice.23
  3.4 0.8 pad_maximum_fusion.turned_ref
  4.2 0.0 copy-done
  4.2 166.5 %shard_map.102 = (bf16[128,4096]{1,0:T(8,128)(2,1)}, bf16[128,4096]{1,0:T(8,128)(2,1)}, bf16[128,4096]{1,0:T(8,128)(2,1)}, f32[256,128]{1,0:T(8,128)}) custom-call(f32[256,128]{1,0:T(8,128)} %pad_maximum_fusion.turned_ref, f32[256,128]{1,0:T(8,128)} %copy-done, bf16[128,256]{1,0:T(8,128)(2,1)} %get-tuple-element.19.ahead_ref, ...), custom_call_target="tpu_custom_call" | custom-call | tf_op jit(solution)/shard_map/pallas_call | solution.py:447
  170.7 1.6 rev.5
  172.3 2.3 %copy.14 = bf16[128,4096]{1,0:T(8,128)(2,1)} copy(bf16[128,4096]{1,0:T(8,128)(2,1)} %get-tuple-element.25) | data formatting | bytes 2097152
  174.6 2.3 %copy.15 = bf16[128,4096]{1,0:T(8,128)(2,1)} copy(bf16[128,4096]{1,0:T(8,128)(2,1)} %get-tuple-element.26) | data formatting | bytes 2097152
  176.9 2.3 %copy.16 = bf16[128,4096]{1,0:T(8,128)(2,1)} copy(bf16[128,4096]{1,0:T(8,128)(2,1)} %get-tuple-element.27) | data formatting | bytes 2097152
  (2 shorter events, 0.0 us)
Async XLA Ops:
  3.1 1.1 copy-start
